TPU v7x, 32 devices: a whole 2x2x4 slice. The times are simulated.
32 devices in a mesh: groups: 2 (over y), blk: 8 (over z, x), uly: 2 (over core).
Axes of the slice: x: 2, y: 2, z: 4, core: 2. Of those that a mesh axis runs over, the one named last changes fastest.
Arguments:
- query: bfloat16 [4096, 1536], P(('groups', 'blk', 'uly')), parts along dimension 0, may hold values from -12 to 12
- key: bfloat16 [4096, 1536], P(('groups', 'blk', 'uly')), parts along dimension 0, may hold values from -6 to 6
- value: bfloat16 [4096, 1536], P(('groups', 'blk', 'uly')), parts along dimension 0, may hold values from -6 to 6
- keep: int32 [64, 28], P(('groups', 'blk')), parts along dimension 0, may hold values from 0 to 1, as said below
Outputs:
- attended: bfloat16 [4096, 1536], P(('groups', 'blk', 'uly')), parts along dimension 0
There are 2 independent parts, one for each index of `groups`. A program takes and returns all parts, laid end to end along the dimension named above; each array names one. Nothing has to cross between parts.
Inputs may be any that keep to these rules, and one draw needn't show every extreme that they name: Tile i has coordinates (i // 8, (i // 2) % 4, i % 2) in the clip's grid of tiles. keep[i, j] refers to key tile (i // 4 - 3) * 4 + j; it is 0 where that tile lies outside the clip, 1 where it is tile i itself, and otherwise 1 exactly when each coordinate differs from tile i's by no more than a per-tile reach of 0 or 1 in that coordinate.
All inputs are finite; a program needn't handle non-finite values.
Results may differ from a plain program's by a relative error of at most 0.0029.
Values may be sent and summed in bfloat16 or wider, within the bound.
A program may use at most 64 MiB of HBM per device.

v0:
```python
import math

import jax
import jax.numpy as jnp
from jax import lax
from jax.sharding import PartitionSpec as P

HD = 128
TILE = 64


neg_fill = -1e30


def from_behind(block, axis, distance):
    devices = range(lax.axis_size(axis))
    route = [(i - distance, i) for i in devices if i - distance in devices]
    return lax.ppermute(block, axis, route)


def band_mask(flags, key_tiles, first_tile):
    width = flags.shape[1]
    column = key_tiles - first_tile
    onehot = (column[None, :] == jnp.arange(width, dtype=jnp.int32)[:, None]).astype(jnp.float32)
    return jnp.dot(flags, onehot, precision=lax.Precision.HIGHEST) > 0.5


def attend(carry, keys, values, key_tiles, queries, flags, first_tile):
    count = keys.shape[0]
    local_heads = queries.shape[1]
    tile_mask = band_mask(flags, key_tiles, first_tile)
    mask = jnp.repeat(tile_mask, TILE, axis=0)[:, None, :]
    scale = 1.0 / math.sqrt(HD)
    peak, total, accum = carry
    keys_h = keys.reshape(count, local_heads, HD)
    values_h = values.reshape(count, local_heads, HD)
    scores = jnp.einsum("qhd,khd->qhk", queries, keys_h, preferred_element_type=jnp.float32) * scale
    masked = jnp.where(mask, scores, neg_fill)
    new_peak = jnp.maximum(peak, jnp.max(masked, axis=2))
    weights = jnp.where(mask, jnp.exp(masked - new_peak[:, :, None]), 0.0)
    factor = jnp.exp(peak - new_peak)
    total = total * factor + jnp.sum(weights, axis=2)
    accum = accum * factor[:, :, None] + jnp.einsum(
        "qhk,khd->qhd", weights.astype(jnp.bfloat16), values_h, preferred_element_type=jnp.float32
    )
    return (new_peak, total, accum)


def body(query, key, value, keep):
    q_loc, k_loc, v_loc = (
        lax.all_to_all(query, "uly", split_axis=1, concat_axis=0, tiled=True),
        lax.all_to_all(key, "uly", split_axis=1, concat_axis=0, tiled=True),
        lax.all_to_all(value, "uly", split_axis=1, concat_axis=0, tiled=True),
    )
    rows = q_loc.shape[0]
    local_heads = q_loc.shape[1] // HD
    tiles_here = rows // TILE
    width = keep.shape[1]
    radius = (width // tiles_here - 1) // 2
    position = lax.axis_index("blk")
    first_tile = (position - radius) * tiles_here
    flags = keep.astype(jnp.float32)
    queries = q_loc.reshape(rows, local_heads, HD)
    initial = (
        jnp.full((rows, local_heads), neg_fill, jnp.float32),
        jnp.zeros((rows, local_heads), jnp.float32),
        jnp.zeros((rows, local_heads, HD), jnp.float32),
    )

    def tiles_of(block):
        return (block * rows + jnp.arange(rows, dtype=jnp.int32)) // TILE

    def step(carry, keys, values, key_tiles):
        return attend(carry, keys, values, key_tiles, queries, flags, first_tile)

    own_pair = jnp.stack((k_loc, v_loc))
    carry = step(initial, k_loc, v_loc, tiles_of(position))
    for distance in range(1, radius + 1):
        moved = [from_behind(own_pair, "blk", sign * distance) for sign in (1, -1)]
        step_carry = carry
        lower = moved[0]
        upper = moved[1]
        step_carry = step(step_carry, lower[0], lower[1], tiles_of(position - distance))
        carry = step(step_carry, upper[0], upper[1], tiles_of(position + distance))
    peak, total, accum = carry
    output = (accum / total[:, :, None]).astype(jnp.bfloat16).reshape(rows, local_heads * HD)
    return lax.all_to_all(output, "uly", split_axis=0, concat_axis=1, tiled=True)


def solution(mesh):
    return jax.shard_map(
        body,
        mesh=mesh,
        in_specs=(
            P(("groups", "blk", "uly"), None),
            P(("groups", "blk", "uly"), None),
            P(("groups", "blk", "uly"), None),
            P(("groups", "blk"), None),
        ),
        out_specs=P(("groups", "blk", "uly"), None),
        check_vma=False,
    )
```

profile of v0, /device:TPU:13, one launch (start us, length us, event | category | flops | bytes accessed | tf_op | source)
XLA Modules:
  0.0 110.6 jit_solution(11380944460250216101)
XLA Ops:
  0.0 2.0 %copy.108 = bf16[128,1536]{0,1:T(8,128)(2,1)} copy(bf16[128,1536]{1,0:T(8,128)(2,1)} %param.5) | data formatting | bytes 786432 | tf_op args[1]
  2.0 4.1 %all-to-all-start = ((bf16[128,2,768]{0,2,1:T(8,128)(2,1)}), bf16[128,2,768]{0,2,1:T(8,128)(2,1)S(1)}, u32[]{:S(2)}, u32[]{:S(2)}) async-start(bf16[128,2,768]{0,2,1:T(8,128)(2,1)} %bitcast.2), calls=%async_computation | async-start | bytes 786432 | tf_op jit(solution)/shard_map/all_to_all | solution.py:52
  6.1 0.9 copy.114
  7.4 3.8 %all-to-all-start.2 = ((bf16[128,2,768]{0,2,1:T(8,128)(2,1)}), bf16[128,2,768]{0,2,1:T(8,128)(2,1)S(1)}, u32[]{:S(2)}, u32[]{:S(2)}) async-start(bf16[128,2,768]{0,2,1:T(8,128)(2,1)} %bitcast.7), calls=%async_computation.2 | async-start | bytes 786432 | tf_op jit(solution)/shard_map/all_to_all | solution.py:53
  13.3 0.8 constant_dynamic-update-slice_fusion
  14.1 1.3 %collective-permute-start.5 = (bf16[2,256,768]{1,2,0:T(8,128)(2,1)}, bf16[2,256,768]{1,2,0:T(8,128)(2,1)S(1)}, u32[]{:S(2)}, u32[]{:S(2)}) collective-permute-start(bf16[2,256,768]{1,2,0:T(8,128)(2,1)} %constant_dynamic-update-slice_fusion), channel_id=1, source_target_pairs={{6,0},{8,2},{10,4},{12,6},{14,8},{7,1},{9,3},{11,5},{13,7},{15,9},... | collective-permute-start | bytes 2359304 | tf_op jit(solution)/shard_map/ppermute | solution.py:18
  15.4 5.8 %collective-permute-start.4 = (bf16[2,256,768]{1,2,0:T(8,128)(2,1)}, bf16[2,256,768]{1,2,0:T(8,128)(2,1)}, u32[]{:S(2)}, u32[]{:S(2)}) collective-permute-start(bf16[2,256,768]{1,2,0:T(8,128)(2,1)} %constant_dynamic-update-slice_fusion), channel_id=1, source_target_pairs={{0,6},{2,8},{4,10},{6,12},{8,14},{1,7},{3,9},{5,11},{7,13},{9,15},... | collective-permute-start | bytes 2359304 | tf_op jit(solution)/shard_map/ppermute | solution.py:18
  21.3 2.0 %collective-permute-start.3 = (bf16[2,256,768]{1,2,0:T(8,128)(2,1)}, bf16[2,256,768]{1,2,0:T(8,128)(2,1)}, u32[]{:S(2)}, u32[]{:S(2)}) collective-permute-start(bf16[2,256,768]{1,2,0:T(8,128)(2,1)} %constant_dynamic-update-slice_fusion), channel_id=1, source_target_pairs={{4,0},{6,2},{8,4},{10,6},{12,8},{14,10},{5,1},{7,3},{9,5},{11,7},{... | collective-permute-start | bytes 2359304 | tf_op jit(solution)/shard_map/ppermute | solution.py:18
  23.3 3.3 %collective-permute-start.2 = (bf16[2,256,768]{1,2,0:T(8,128)(2,1)}, bf16[2,256,768]{1,2,0:T(8,128)(2,1)}, u32[]{:S(2)}, u32[]{:S(2)}) collective-permute-start(bf16[2,256,768]{1,2,0:T(8,128)(2,1)} %constant_dynamic-update-slice_fusion), channel_id=1, source_target_pairs={{0,4},{2,6},{4,8},{6,10},{8,12},{10,14},{1,5},{3,7},{5,9},{7,11},{... | collective-permute-start | bytes 2359304 | tf_op jit(solution)/shard_map/ppermute | solution.py:18
  26.6 3.1 %collective-permute-start = (bf16[2,256,768]{1,2,0:T(8,128)(2,1)}, bf16[2,256,768]{1,2,0:T(8,128)(2,1)}, u32[]{:S(2)}, u32[]{:S(2)}) collective-permute-start(bf16[2,256,768]{1,2,0:T(8,128)(2,1)} %constant_dynamic-update-slice_fusion), channel_id=1, source_target_pairs={{0,2},{2,4},{4,6},{6,8},{8,10},{10,12},{12,14},{1,3},{3,5},{5,7},{... | collective-permute-start | bytes 2359304 | tf_op jit(solution)/shard_map/ppermute | solution.py:18
  29.7 0.9 copy.110
  30.6 5.1 %all-to-all-start.1 = ((bf16[128,2,768]{0,2,1:T(8,128)(2,1)}), bf16[128,2,768]{0,2,1:T(8,128)(2,1)S(1)}, u32[]{:S(2)}, u32[]{:S(2)}) async-start(bf16[128,2,768]{0,2,1:T(8,128)(2,1)} %bitcast.4), calls=%async_computation.1 | async-start | bytes 786432 | tf_op jit(solution)/shard_map/all_to_all | solution.py:51
  39.8 12.7 %collective-permute-start.1 = (bf16[2,256,768]{1,2,0:T(8,128)(2,1)}, bf16[2,256,768]{1,2,0:T(8,128)(2,1)S(1)}, u32[]{:S(2)}, u32[]{:S(2)}) collective-permute-start(bf16[2,256,768]{1,2,0:T(8,128)(2,1)} %constant_dynamic-update-slice_fusion), channel_id=1, source_target_pairs={{2,0},{4,2},{6,4},{8,6},{10,8},{12,10},{14,12},{3,1},{5,3},{7,5},{... | collective-permute-start | bytes 2359304 | tf_op jit(solution)/shard_map/ppermute | solution.py:18
  52.5 1.2 %fusion.99 = (bf16[1,256,768]{1,2,0:T(8,128)(2,1)S(1)}, bf16[1,256,768]{1,2,0:T(8,128)(2,1)S(1)}) fusion(bf16[2,256,768]{1,2,0:T(8,128)(2,1)} %collective-permute-done.4), kind=kLoop, calls=%fused_computation.165 | loop fusion | bytes 1572864 | tf_op jit(solution)/shard_map/slice | solution.py:83
  53.7 17.0 %collective-permute-done.2 = bf16[2,256,768]{1,2,0:T(8,128)(2,1)} collective-permute-done((bf16[2,256,768]{1,2,0:T(8,128)(2,1)}, bf16[2,256,768]{1,2,0:T(8,128)(2,1)}, u32[]{:S(2)}, u32[]{:S(2)}) %collective-permute-start.2) | collective-permute-done | bytes 786464 | tf_op jit(solution)/shard_map/ppermute | solution.py:18
  70.6 1.2 %fusion.97 = (bf16[1,256,768]{1,2,0:T(8,128)(2,1)S(1)}, bf16[1,256,768]{1,2,0:T(8,128)(2,1)S(1)}) fusion(bf16[2,256,768]{1,2,0:T(8,128)(2,1)} %collective-permute-done.2), kind=kLoop, calls=%fused_computation.163 | loop fusion | bytes 1572864 | tf_op jit(solution)/shard_map/slice | solution.py:83
  71.8 15.5 %collective-permute-done = bf16[2,256,768]{1,2,0:T(8,128)(2,1)} collective-permute-done((bf16[2,256,768]{1,2,0:T(8,128)(2,1)}, bf16[2,256,768]{1,2,0:T(8,128)(2,1)}, u32[]{:S(2)}, u32[]{:S(2)}) %collective-permute-start) | collective-permute-done | bytes 786464 | tf_op jit(solution)/shard_map/ppermute | solution.py:18
  87.3 1.2 %fusion.95 = (bf16[1,256,768]{1,2,0:T(8,128)(2,1)S(1)}, bf16[1,256,768]{1,2,0:T(8,128)(2,1)S(1)}) fusion(bf16[2,256,768]{1,2,0:T(8,128)(2,1)} %collective-permute-done), kind=kLoop, calls=%fused_computation.161 | loop fusion | bytes 1572864 | tf_op jit(solution)/shard_map/slice | solution.py:83
  88.9 4.1 %collective-permute-done.1 = bf16[2,256,768]{1,2,0:T(8,128)(2,1)S(1)} collective-permute-done((bf16[2,256,768]{1,2,0:T(8,128)(2,1)}, bf16[2,256,768]{1,2,0:T(8,128)(2,1)S(1)}, u32[]{:S(2)}, u32[]{:S(2)}) %collective-permute-start.1) | collective-permute-done | bytes 786464 | tf_op jit(solution)/shard_map/ppermute | solution.py:18
  94.0 1.2 %fusion.98 = (bf16[1,256,768]{1,2,0:T(8,128)(2,1)S(1)}, bf16[1,256,768]{1,2,0:T(8,128)(2,1)S(1)}) fusion(bf16[2,256,768]{1,2,0:T(8,128)(2,1)} %collective-permute-done.3), kind=kLoop, calls=%fused_computation.164 | loop fusion | bytes 1572864 | tf_op jit(solution)/shard_map/slice | solution.py:84
  101.5 0.9 fusion.1
  102.4 2.0 %fusion.28 = bf16[256,6,128]{2,0,1:T(8,128)(2,1)S(1)} fusion(f32[256,6,128]{2,0,1:T(8,128)S(1)} %convolution_bitcast_fusion, f32[256,6,128]{2,0,1:T(8,128)S(1)} %convolution_bitcast_fusion.1, f32[256,6,128]{2,0,1:T(8,128)S(1)} %convolution_bitcast_fusion.2, f32[256,6,128]{2,0,1:T(8,128)S(1)} %convolution_bitcast_fusion.3, ...), kind=kOutput, calls=%fused_computation.49 | convolution fusion | flops 104398848 | bytes 7186432 | tf_op jit(solution)/shard_map/qhk,khd->qhd/dot_general | solution.py:43
  104.8 4.8 %all_to_all.67 = bf16[2,128,768]{1,2,0:T(8,128)(2,1)S(1)} all-to-all(bf16[2,128,768]{1,2,0:T(8,128)(2,1)S(1)} %copy.151), channel_id=1, replica_groups=mesh['groups'=2,'blk'=8,'uly'=2] {'uly'}, dimensions={0} | all-to-all | bytes 786432 | tf_op jit(solution)/shard_map/all_to_all | solution.py:87
  109.6 0.9 copy.152
  (72 shorter events, 14.4 us)
Async XLA Ops:
  0.0 6.1 %copy-start = (bf16[128,1536]{1,0:T(8,128)(2,1)S(1)}, bf16[128,1536]{1,0:T(8,128)(2,1)}, u32[]{:S(2)}) copy-start(bf16[128,1536]{1,0:T(8,128)(2,1)} %param.6) | copy-start | bytes 1179652
  2.0 5.4 %all-to-all-start = ((bf16[128,2,768]{0,2,1:T(8,128)(2,1)}), bf16[128,2,768]{0,2,1:T(8,128)(2,1)S(1)}, u32[]{:S(2)}, u32[]{:S(2)}) async-start(bf16[128,2,768]{0,2,1:T(8,128)(2,1)} %bitcast.2), calls=%async_computation | async-start | bytes 786432 | tf_op jit(solution)/shard_map/all_to_all | solution.py:52
  7.4 5.3 %all-to-all-start.2 = ((bf16[128,2,768]{0,2,1:T(8,128)(2,1)}), bf16[128,2,768]{0,2,1:T(8,128)(2,1)S(1)}, u32[]{:S(2)}, u32[]{:S(2)}) async-start(bf16[128,2,768]{0,2,1:T(8,128)(2,1)} %bitcast.7), calls=%async_computation.2 | async-start | bytes 786432 | tf_op jit(solution)/shard_map/all_to_all | solution.py:53
  11.9 17.8 %copy-start.1 = (bf16[128,1536]{1,0:T(8,128)(2,1)S(1)}, bf16[128,1536]{1,0:T(8,128)(2,1)}, u32[]{:S(2)}) copy-start(bf16[128,1536]{1,0:T(8,128)(2,1)} %param.4) | copy-start | bytes 1179652
  13.1 22.6 %copy-start.2 = (s32[4,28]{1,0:T(4,128)S(1)}, s32[4,28]{1,0:T(4,128)}, u32[]{:S(2)}) copy-start(s32[4,28]{1,0:T(4,128)} %param.7) | copy-start | bytes 1348
  14.1 82.0 %collective-permute-start.5 = (bf16[2,256,768]{1,2,0:T(8,128)(2,1)}, bf16[2,256,768]{1,2,0:T(8,128)(2,1)S(1)}, u32[]{:S(2)}, u32[]{:S(2)}) collective-permute-start(bf16[2,256,768]{1,2,0:T(8,128)(2,1)} %constant_dynamic-update-slice_fusion), channel_id=1, source_target_pairs={{6,0},{8,2},{10,4},{12,6},{14,8},{7,1},{9,3},{11,5},{13,7},{15,9},... | collective-permute-start | bytes 2359304 | tf_op jit(solution)/shard_map/ppermute | solution.py:18
  15.4 24.4 %collective-permute-start.4 = (bf16[2,256,768]{1,2,0:T(8,128)(2,1)}, bf16[2,256,768]{1,2,0:T(8,128)(2,1)}, u32[]{:S(2)}, u32[]{:S(2)}) collective-permute-start(bf16[2,256,768]{1,2,0:T(8,128)(2,1)} %constant_dynamic-update-slice_fusion), channel_id=1, source_target_pairs={{0,6},{2,8},{4,10},{6,12},{8,14},{1,7},{3,9},{5,11},{7,13},{9,15},... | collective-permute-start | bytes 2359304 | tf_op jit(solution)/shard_map/ppermute | solution.py:18
  21.3 72.7 %collective-permute-start.3 = (bf16[2,256,768]{1,2,0:T(8,128)(2,1)}, bf16[2,256,768]{1,2,0:T(8,128)(2,1)}, u32[]{:S(2)}, u32[]{:S(2)}) collective-permute-start(bf16[2,256,768]{1,2,0:T(8,128)(2,1)} %constant_dynamic-update-slice_fusion), channel_id=1, source_target_pairs={{4,0},{6,2},{8,4},{10,6},{12,8},{14,10},{5,1},{7,3},{9,5},{11,7},{... | collective-permute-start | bytes 2359304 | tf_op jit(solution)/shard_map/ppermute | solution.py:18
  23.3 47.3 %collective-permute-start.2 = (bf16[2,256,768]{1,2,0:T(8,128)(2,1)}, bf16[2,256,768]{1,2,0:T(8,128)(2,1)}, u32[]{:S(2)}, u32[]{:S(2)}) collective-permute-start(bf16[2,256,768]{1,2,0:T(8,128)(2,1)} %constant_dynamic-update-slice_fusion), channel_id=1, source_target_pairs={{0,4},{2,6},{4,8},{6,10},{8,12},{10,14},{1,5},{3,7},{5,9},{7,11},{... | collective-permute-start | bytes 2359304 | tf_op jit(solution)/shard_map/ppermute | solution.py:18
  26.6 60.7 %collective-permute-start = (bf16[2,256,768]{1,2,0:T(8,128)(2,1)}, bf16[2,256,768]{1,2,0:T(8,128)(2,1)}, u32[]{:S(2)}, u32[]{:S(2)}) collective-permute-start(bf16[2,256,768]{1,2,0:T(8,128)(2,1)} %constant_dynamic-update-slice_fusion), channel_id=1, source_target_pairs={{0,2},{2,4},{4,6},{6,8},{8,10},{10,12},{12,14},{1,3},{3,5},{5,7},{... | collective-permute-start | bytes 2359304 | tf_op jit(solution)/shard_map/ppermute | solution.py:18
  30.6 8.0 %all-to-all-start.1 = ((bf16[128,2,768]{0,2,1:T(8,128)(2,1)}), bf16[128,2,768]{0,2,1:T(8,128)(2,1)S(1)}, u32[]{:S(2)}, u32[]{:S(2)}) async-start(bf16[128,2,768]{0,2,1:T(8,128)(2,1)} %bitcast.4), calls=%async_computation.1 | async-start | bytes 786432 | tf_op jit(solution)/shard_map/all_to_all | solution.py:51
  39.8 53.2 %collective-permute-start.1 = (bf16[2,256,768]{1,2,0:T(8,128)(2,1)}, bf16[2,256,768]{1,2,0:T(8,128)(2,1)S(1)}, u32[]{:S(2)}, u32[]{:S(2)}) collective-permute-start(bf16[2,256,768]{1,2,0:T(8,128)(2,1)} %constant_dynamic-update-slice_fusion), channel_id=1, source_target_pairs={{2,0},{4,2},{6,4},{8,6},{10,8},{12,10},{14,12},{3,1},{5,3},{7,5},{... | collective-permute-start | bytes 2359304 | tf_op jit(solution)/shard_map/ppermute | solution.py:18
where the time goes:
time: 111 us
  starting transfers between devices  41.2 us (37%)
  waiting for transfers between devices  36.9 us (33%)
  local copies, waits for them, and re-layouts  15.2 us (14%)
  matrix products  9.73 us (9%)
  blocking collectives  4.84 us (4%)
  other arithmetic  2.19 us (2%)
    ppermute x6, waiting for transfers between devices, from_behind(): return lax.ppermute(block, axis, route)  36.6 us
    ppermute x6, starting transfers between devices, from_behind(): return lax.ppermute(block, axis, route)  28.2 us
    dot_general x7, matrix products, attend(): jnp.einsum('qhk,khd->qhd', weights.astype(jnp.bfloat16), values_h, prefer...  5.62 us
    all_to_all x1, starting transfers between devices, body(): lax.all_to_all(query, 'uly', split_axis=1, concat_axis=0, tiled=True)  5.06 us
    all_to_all x1, blocking collectives, body(): lax.all_to_all(output, 'uly', split_axis=0, concat_axis=1, tiled=True)  4.84 us
    unnamed x10, local copies, waits for them, and re-layouts  4.57 us
    all_to_all x1, starting transfers between devices, body(): lax.all_to_all(key, 'uly', split_axis=1, concat_axis=0, tiled=True)  4.13 us
    all_to_all x1, starting transfers between devices, body(): lax.all_to_all(value, 'uly', split_axis=1, concat_axis=0, tiled=True)  3.83 us
  transfers between devices with their start and end apart: 9, of which 4 were waited for; matrix products, arithmetic and copies ran while one was open for 13% of the time, Pallas kernels for 0%

commit v1 on v0

v1 whole, which is shorter than its diff:
```python
import functools
import math

import jax
import jax.numpy as jnp
from jax import lax
from jax.experimental import pallas as pl
from jax.experimental.pallas import tpu as pltpu
from jax.sharding import PartitionSpec as P

HD = 128
TILE = 64
FAR = 1e30
F32 = jnp.float32
BF16 = jnp.bfloat16
MESH = pl.DeviceIdType.MESH


def kernel(heads, frames, query, key, value, keep, out,
           kv, kvs, qs, q2, fq, fkeep, bias, fbias, ps, pr, accs, peaks, totals, o2,
           sem_kvs, sem_qs, sem_own, sem_own_q, recv_kv, zsend, psend, pqsend, recv_q2,
           fqsend, recv_fq, ksend, recv_keep, part_send, part_recv, out_local, out_send, out_recv):
    half = heads // 2
    group = lax.axis_index("groups")
    b = lax.axis_index("blk")
    u = lax.axis_index("uly")
    t = b // 2
    s = b - 2 * t
    other = 1 - u
    facing = 1 - s
    across = b + 1 - 2 * s
    has_low = t > 0
    has_high = t < frames - 1

    def dev(blk, core):
        return (group, blk, core)

    def remote(src, dst, send, recv, device):
        return pltpu.make_async_remote_copy(
            src_ref=src, dst_ref=dst, send_sem=send, recv_sem=recv,
            device_id=device, device_id_type=MESH)

    def columns(head):
        return pl.ds(pl.multiple_of(head * HD, HD), HD)

    def load_key(hd):
        return pltpu.make_async_copy(key.at[:, columns(hd)], kvs.at[hd, 0], sem_kvs.at[hd, 0])

    def load_value(hd):
        return pltpu.make_async_copy(value.at[:, columns(hd)], kvs.at[hd, 1], sem_kvs.at[hd, 1])

    def load_query(hd):
        return pltpu.make_async_copy(query.at[:, columns(hd)], qs.at[hd], sem_qs.at[hd])

    def own_kv(h):
        return (
            pltpu.make_async_copy(key.at[:, columns(u * half + h)], kv.at[h, 2 + u, 0], sem_own.at[h, 0]),
            pltpu.make_async_copy(value.at[:, columns(u * half + h)], kv.at[h, 2 + u, 1], sem_own.at[h, 1]),
        )

    def own_q(h):
        return pltpu.make_async_copy(query.at[:, columns(u * half + h)], q2.at[h, u], sem_own_q.at[h])

    for h in range(half):
        for c in range(2):
            load_key(c * half + h).start()
            load_value(c * half + h).start()
            load_query(c * half + h).start()
    for h in range(half):
        for copy in own_kv(h):
            copy.start()
        own_q(h).start()

    def to_high(c, h):
        return remote(kvs.at[c * half + h], kv.at[h, u], zsend.at[0, c, h], recv_kv.at[u, h], dev(b + 2, c))

    def to_low(c, h):
        return remote(kvs.at[c * half + h], kv.at[h, 4 + u], zsend.at[1, c, h], recv_kv.at[4 + u, h], dev(b - 2, c))

    def got_kv(row, h):
        return remote(kvs.at[h], kv.at[h, row], zsend.at[0, 0, h], recv_kv.at[row, h], dev(b, other))

    def to_partner_kv():
        return remote(kvs.at[pl.ds(other * half, half)], kv.at[:, 2 + u], psend.at[0], psend.at[1], dev(b, other))

    def got_partner_kv():
        return remote(kvs.at[pl.ds(other * half, half)], kv.at[:, 2 + other], psend.at[0], psend.at[1], dev(b, other))

    def to_partner_q():
        return remote(qs.at[pl.ds(other * half, half)], q2.at[:, u], pqsend.at[0], recv_q2.at[0], dev(b, other))

    def got_partner_q():
        return remote(qs.at[pl.ds(other * half, half)], q2.at[:, other], pqsend.at[0], recv_q2.at[0], dev(b, other))

    def to_across_q(c, h):
        return remote(qs.at[c * half + h], fq.at[h], fqsend.at[c, h], recv_fq.at[h], dev(across, c))

    def to_across_keep():
        return remote(keep, fkeep, ksend.at[0], recv_keep.at[0], dev(across, u))

    def part(h):
        return remote(ps.at[h], pr.at[h], part_send.at[h], part_recv.at[h], dev(across, u))

    barrier = pltpu.get_barrier_semaphore()

    def greet(blk, core):
        pl.semaphore_signal(barrier, inc=1, device_id=dev(blk, core), device_id_type=MESH)

    greet(b, other)
    for c in range(2):
        greet(across, c)

        @pl.when(has_low)
        def _(c=c):
            greet(b - 2, c)

        @pl.when(has_high)
        def _(c=c):
            greet(b + 2, c)

    @pl.when(jnp.logical_not(has_low))
    def _():
        kv[:, 0:2] = jnp.zeros((half, 2, 2, HD, HD), BF16)

    @pl.when(jnp.logical_not(has_high))
    def _():
        kv[:, 4:6] = jnp.zeros((half, 2, 2, HD, HD), BF16)

    around = jnp.where(has_low, 2, 0) + jnp.where(has_high, 2, 0)
    pl.semaphore_wait(barrier, 3 + around)

    to_across_keep().start()
    for h in range(half):
        for c in range(2):
            load_key(c * half + h).wait()
            load_value(c * half + h).wait()

            @pl.when(has_high)
            def _(c=c, h=h):
                to_high(c, h).start()

            @pl.when(has_low)
            def _(c=c, h=h):
                to_low(c, h).start()

            load_query(c * half + h).wait()

            @pl.when(u == facing)
            def _(c=c, h=h):
                to_across_q(c, h).start()

    to_partner_kv().start()
    to_partner_q().start()
    for h in range(half):
        for copy in own_kv(h):
            copy.wait()
        own_q(h).wait()

    wide = keep.shape[1]
    tiles_here = keep.shape[0]
    reach = (wide // tiles_here - 1) // 2

    def addend(flags, column, count):
        lanes = lax.broadcasted_iota(jnp.int32, (wide, count), 1)
        chosen = lax.broadcasted_iota(jnp.int32, (wide, count), 0) == column(lanes)
        picked = jnp.dot(flags.astype(F32).astype(BF16), chosen.astype(F32).astype(BF16), preferred_element_type=F32)
        return jnp.where(picked > 0.5, 0.0, -FAR)

    def own_column(lanes):
        row = lanes // HD
        return (tiles_here * (reach - 2) + 2 * tiles_here * (row // 2)
                + 2 * (row % 2) + (lanes % HD) // TILE)

    def far_column(lanes):
        return (tiles_here * (reach - 2 + 2 * s - 1) + 2 * tiles_here * (lanes // HD)
                + 2 * facing + (lanes % HD) // TILE)

    bias[...] = addend(keep[...], own_column, 6 * HD)
    remote(keep, fkeep, ksend.at[0], recv_keep.at[0], dev(across, u)).wait_recv()
    fbias[...] = addend(fkeep[...], far_column, 3 * HD)

    got_partner_kv().wait_recv()
    got_partner_q().wait_recv()

    scale = math.log2(math.e) / math.sqrt(HD)
    nt = (((1,), (1,)), ((), ()))

    def softmax(scores, rows, addends):
        ms, ls, ws = [], [], []
        for i in range(rows // TILE):
            x = scores[i * TILE:(i + 1) * TILE] * scale + addends[i]
            m = jnp.max(x, axis=1, keepdims=True)
            w = jnp.exp2(x - m)
            ls.append(jnp.sum(w, axis=1, keepdims=True))
            ms.append(m)
            ws.append(w.astype(BF16))
        return jnp.concatenate(ms, 0), jnp.concatenate(ls, 0), jnp.concatenate(ws, 0)

    def far(h):
        k = jnp.concatenate([kv[h, 2 * i + facing, 0] for i in range(3)], 0)
        v = jnp.concatenate([kv[h, 2 * i + facing, 1] for i in range(3)], 0)
        scores = lax.dot_general(fq[h], k, nt, preferred_element_type=F32)
        m, l, w = softmax(scores, HD, [fbias[pl.ds(2 * s + i, 1), :] for i in range(2)])
        ps[h, 0:HD, :] = jnp.dot(w, v, preferred_element_type=F32)
        lane = lax.broadcasted_iota(jnp.int32, (HD, HD), 1)
        ps[h, HD:HD + 8, :] = jnp.where(lane == 0, m, l).T[0:8, :]
        part(h).start()

    def near(h):
        k = kv[h, :, 0].reshape(6 * HD, HD)
        v = kv[h, :, 1].reshape(6 * HD, HD)
        scores = lax.dot_general(q2[h].reshape(2 * HD, HD), k, nt, preferred_element_type=F32)
        m, l, w = softmax(scores, 2 * HD, [bias[i:i + 1, :] for i in range(4)])
        accs[h] = jnp.dot(w, v, preferred_element_type=F32).reshape(2, HD, HD)
        peaks[h] = jnp.broadcast_to(m, (2 * HD, HD)).reshape(2, HD, HD)
        totals[h] = jnp.broadcast_to(l, (2 * HD, HD)).reshape(2, HD, HD)

    def keep_out(h):
        return pltpu.make_async_copy(o2.at[h, u], out.at[:, columns(u * half + h)], out_local.at[h])

    def give_out(h):
        return remote(o2.at[h, other], out.at[:, columns(u * half + h)], out_send.at[h], out_recv.at[h], dev(b, other))

    def got_out(h):
        return remote(o2.at[h, other], out.at[:, columns(other * half + h)], out_send.at[h], out_recv.at[h], dev(b, other))

    def merge(h):
        o2[h, s] = (accs[h, s] / totals[h, s]).astype(BF16)
        part(h).wait_recv()
        stats = jnp.concatenate([pr[h, HD:HD + 8, :]] * 16, 0).T
        m2, l2 = stats[:, 0:1], stats[:, 1:2]
        m1 = peaks[h, facing]
        m = jnp.maximum(m1, m2)
        a1, a2 = jnp.exp2(m1 - m), jnp.exp2(m2 - m)
        mixed = accs[h, facing] * a1 + pr[h, 0:HD, :] * a2
        o2[h, facing] = (mixed / (totals[h, facing] * a1 + l2 * a2)).astype(BF16)
        give_out(h).start()
        keep_out(h).start()

    def step(h, carry):
        for r in range(2):
            @pl.when(has_low)
            def _(r=r):
                got_kv(r, h).wait_recv()

            @pl.when(has_high)
            def _(r=r):
                got_kv(4 + r, h).wait_recv()

        to_across_q(0, h).wait_recv()
        far(h)
        near(h)

        @pl.when(h > 0)
        def _():
            merge(h - 1)

        return carry

    lax.fori_loop(0, half, step, 0)
    merge(half - 1)

    to_across_keep().wait_send()
    to_partner_kv().wait_send()
    to_partner_q().wait_send()
    for h in range(half):
        for c in range(2):
            @pl.when(has_high)
            def _(c=c, h=h):
                to_high(c, h).wait_send()

            @pl.when(has_low)
            def _(c=c, h=h):
                to_low(c, h).wait_send()

            @pl.when(u == facing)
            def _(c=c, h=h):
                to_across_q(c, h).wait_send()

        part(h).wait_send()
        keep_out(h).wait()
        give_out(h).wait_send()
        got_out(h).wait_recv()


def body(query, key, value, keep):
    rows, width = query.shape
    heads = width // HD
    half = heads // 2
    frames = lax.axis_size("blk") // 2
    tiles, span = keep.shape
    dma = pltpu.SemaphoreType.DMA
    anywhere = pl.BlockSpec(memory_space=pl.ANY)
    scratch = [
        pltpu.VMEM((half, 6, 2, HD, HD), BF16),
        pltpu.VMEM((heads, 2, HD, HD), BF16),
        pltpu.VMEM((heads, HD, HD), BF16),
        pltpu.VMEM((half, 2, HD, HD), BF16),
        pltpu.VMEM((half, HD, HD), BF16),
        pltpu.VMEM((tiles, span), jnp.int32),
        pltpu.VMEM((tiles, 6 * HD), F32),
        pltpu.VMEM((tiles, 3 * HD), F32),
        pltpu.VMEM((half, HD + 8, HD), F32),
        pltpu.VMEM((half, HD + 8, HD), F32),
        pltpu.VMEM((half, 2, HD, HD), F32),
        pltpu.VMEM((half, 2, HD, HD), F32),
        pltpu.VMEM((half, 2, HD, HD), F32),
        pltpu.VMEM((half, 2, HD, HD), BF16),
        dma((heads, 2)),
        dma((heads,)),
        dma((half, 2)),
        dma((half,)),
        dma((6, half)),
        dma((2, 2, half)),
        dma((2,)),
        dma((1,)),
        dma((1,)),
        dma((2, half)),
        dma((half,)),
        dma((1,)),
        dma((1,)),
        dma((half,)),
        dma((half,)),
        dma((half,)),
        dma((half,)),
        dma((half,)),
    ]
    return pl.pallas_call(
        functools.partial(kernel, heads, frames),
        out_shape=jax.ShapeDtypeStruct((rows, width), BF16),
        in_specs=[anywhere, anywhere, anywhere, pl.BlockSpec(memory_space=pltpu.VMEM)],
        out_specs=anywhere,
        scratch_shapes=scratch,
        compiler_params=pltpu.CompilerParams(
            collective_id=0, has_side_effects=True, vmem_limit_bytes=56 * 1024 * 1024),
    )(query, key, value, keep)


def solution(mesh):
    return jax.shard_map(
        body,
        mesh=mesh,
        in_specs=(
            P(("groups", "blk", "uly"), None),
            P(("groups", "blk", "uly"), None),
            P(("groups", "blk", "uly"), None),
            P(("groups", "blk"), None),
        ),
        out_specs=P(("groups", "blk", "uly"), None),
        check_vma=False,
    )
```

time: 111 us -> 32.2 us (0.29)
  the two profiles are of different devices: /device:TPU:13 before, /device:TPU:0 now
where the time goes in v1:
time: 32.2 us; the launch traced here: 31.9 us
  Pallas kernels  30.2 us (94%)
  local copies, waits for them, and re-layouts  1.77 us (5%)
    pallas_call x1, Pallas kernels, body(): pl.pallas_call(functools.partial(kernel, heads, frames), out_shape=jax.Sh...  30.2 us
    unnamed x1, local copies, waits for them, and re-layouts  1.77 us

profile of v1, /device:TPU:0, one launch (start us, length us, event | category | flops | bytes accessed | tf_op | source)
XLA Modules:
  0.0 31.9 jit_solution(8730100213034198058)
XLA Ops:
  0.0 30.2 %shard_map.46 = bf16[128,1536]{1,0:T(8,128)(2,1)} custom-call(bf16[128,1536]{1,0:T(8,128)(2,1)} %query.1, bf16[128,1536]{1,0:T(8,128)(2,1)} %key.1, bf16[128,1536]{1,0:T(8,128)(2,1)} %value.1, s32[4,28]{1,0:T(4,128)} %keep.1), custom_call_target="tpu_custom_call" | custom-call | tf_op jit(solution)/shard_map/pallas_call | solution.py:328
  30.2 1.8 %copy.6 = bf16[128,1536]{1,0:T(8,128)(2,1)} copy(bf16[128,1536]{1,0:T(8,128)(2,1)} %shard_map.46) | data formatting | bytes 786432

commit v2 on v1

--- a/solution.py
+++ b/solution.py
@@ -11,6 +11,7 @@
 HD = 128
 TILE = 64
 FAR = 1e30
+LEAD = 4
 F32 = jnp.float32
 BF16 = jnp.bfloat16
 MESH = pl.DeviceIdType.MESH
@@ -129,19 +130,24 @@
     around = jnp.where(has_low, 2, 0) + jnp.where(has_high, 2, 0)
     pl.semaphore_wait(barrier, 3 + around)
 
+    def send_kv(c, h):
+        @pl.when(has_high)
+        def _():
+            to_high(c, h).start()
+
+        @pl.when(has_low)
+        def _():
+            to_low(c, h).start()
+
     to_across_keep().start()
     for h in range(half):
         for c in range(2):
             load_key(c * half + h).wait()
             load_value(c * half + h).wait()
 
-            @pl.when(has_high)
-            def _(c=c, h=h):
-                to_high(c, h).start()
-
-            @pl.when(has_low)
-            def _(c=c, h=h):
-                to_low(c, h).start()
+            @pl.when(u == facing)
+            def _(c=c, h=h):
+                send_kv(c, h)
 
             load_query(c * half + h).wait()
 
@@ -237,28 +243,43 @@
         give_out(h).start()
         keep_out(h).start()
 
-    def step(h, carry):
-        for r in range(2):
-            @pl.when(has_low)
-            def _(r=r):
-                got_kv(r, h).wait_recv()
-
-            @pl.when(has_high)
-            def _(r=r):
-                got_kv(4 + r, h).wait_recv()
-
+    def await_row(row, h):
+        @pl.when(has_low)
+        def _():
+            got_kv(row, h).wait_recv()
+
+        @pl.when(has_high)
+        def _():
+            got_kv(4 + row, h).wait_recv()
+
+    def border(h):
+        await_row(facing, h)
         to_across_q(0, h).wait_recv()
         far(h)
+
+    def lead(h, carry):
+        border(h)
+        return carry
+
+    def step(h, carry):
+        @pl.when(h + LEAD < half)
+        def _():
+            border(h + LEAD)
+
+        await_row(s, h)
         near(h)
-
-        @pl.when(h > 0)
-        def _():
-            merge(h - 1)
-
+        merge(h)
         return carry
 
+    lax.fori_loop(0, LEAD, lead, 0)
+
+    @pl.when(u != facing)
+    def _():
+        for h in range(half):
+            for c in range(2):
+                send_kv(c, h)
+
     lax.fori_loop(0, half, step, 0)
-    merge(half - 1)
 
     to_across_keep().wait_send()
     to_partner_kv().wait_send()

time: 32.2 us -> 28.7 us (0.89)
  Pallas kernels: 30.2 us -> 26.7 us
    pallas_call x1, Pallas kernels: 30.2 us -> 26.7 us  [body(): pl.pallas_call(functools.partial(kernel, heads, frames), out_shape=jax.Sh...]
where the time goes in v2:
time: 28.7 us; the launch traced here: 28.5 us
  Pallas kernels  26.7 us (93%)
  local copies, waits for them, and re-layouts  1.77 us (6%)
    pallas_call x1, Pallas kernels, body(): pl.pallas_call(functools.partial(kernel, heads, frames), out_shape=jax.Sh...  26.7 us
    unnamed x1, local copies, waits for them, and re-layouts  1.77 us

profile of v2, /device:TPU:0, one launch (start us, length us, event | category | flops | bytes accessed | tf_op | source)
XLA Modules:
  0.0 28.5 jit_solution(10290430652632507294)
XLA Ops:
  0.0 26.7 %shard_map.46 = bf16[128,1536]{1,0:T(8,128)(2,1)} custom-call(bf16[128,1536]{1,0:T(8,128)(2,1)} %query.1, bf16[128,1536]{1,0:T(8,128)(2,1)} %key.1, bf16[128,1536]{1,0:T(8,128)(2,1)} %value.1, s32[4,28]{1,0:T(4,128)} %keep.1), custom_call_target="tpu_custom_call" | custom-call | tf_op jit(solution)/shard_map/pallas_call | solution.py:349
  26.7 1.8 %copy.6 = bf16[128,1536]{1,0:T(8,128)(2,1)} copy(bf16[128,1536]{1,0:T(8,128)(2,1)} %shard_map.46) | data formatting | bytes 786432

commit v3 on v2

--- a/solution.py
+++ b/solution.py
@@ -348,9 +348,9 @@
     ]
     return pl.pallas_call(
         functools.partial(kernel, heads, frames),
-        out_shape=jax.ShapeDtypeStruct((rows, width), BF16),
+        out_shape=pltpu.VMEM((rows, width), BF16),
         in_specs=[anywhere, anywhere, anywhere, pl.BlockSpec(memory_space=pltpu.VMEM)],
-        out_specs=anywhere,
+        out_specs=pl.BlockSpec(memory_space=pltpu.VMEM),
         scratch_shapes=scratch,
         compiler_params=pltpu.CompilerParams(
             collective_id=0, has_side_effects=True, vmem_limit_bytes=56 * 1024 * 1024),

time: 28.7 us -> 27.6 us (0.962)
  local copies, waits for them, and re-layouts: 1.77 us -> 0.75 us
    unnamed x1, local copies, waits for them, and re-layouts: 1.77 us -> 0.75 us
where the time goes in v3:
time: 27.6 us; the launch traced here: 27.3 us
  Pallas kernels  26.6 us (96%)
  local copies, waits for them, and re-layouts  0.75 us (3%)
    pallas_call x1, Pallas kernels, body(): pl.pallas_call(functools.partial(kernel, heads, frames), out_shape=pltpu....  26.6 us
    unnamed x1, local copies, waits for them, and re-layouts  0.75 us

profile of v3, /device:TPU:0, one launch (start us, length us, event | category | flops | bytes accessed | tf_op | source)
XLA Modules:
  0.0 27.3 jit_solution(9277031072517362158)
XLA Ops:
  0.0 26.6 %shard_map.46 = bf16[128,1536]{1,0:T(8,128)(2,1)S(1)} custom-call(bf16[128,1536]{1,0:T(8,128)(2,1)} %query.1, bf16[128,1536]{1,0:T(8,128)(2,1)} %key.1, bf16[128,1536]{1,0:T(8,128)(2,1)} %value.1, s32[4,28]{1,0:T(4,128)} %keep.1), custom_call_target="tpu_custom_call" | custom-call | tf_op jit(solution)/shard_map/pallas_call | solution.py:349
  26.6 0.7 %copy.6 = bf16[128,1536]{1,0:T(8,128)(2,1)} copy(bf16[128,1536]{1,0:T(8,128)(2,1)S(1)} %shard_map.46) | data formatting | bytes 786432
